TPU v7x, 32 devices: a whole 2x2x4 slice. The times are simulated.
32 devices in a mesh: row: 4 (over x, core), col: 8 (over z, y).
Axes of the slice: x: 2, y: 2, z: 4, core: 2. Of those that a mesh axis runs over, the one named last changes fastest.
Arguments:
- points: bfloat16 [12, 4, 512, 64], P(None, 'row', 'col'), may hold values from -7.5 to 7.5
- inverse_factor: bfloat16 [512, 512], replicated, as said below
- panel_index: int32 [1], replicated, may hold values from 3 to 23
- column_map: int32 [8], P('col'), may hold values from 0 to 7, each once
Outputs:
- panel: bfloat16 [6, 4, 512, 512], P(None, 'row', 'col')
- update: bfloat16 [6, 4, 512, 8, 512], P(None, 'row', None, 'col')
Inputs may be any that keep to these rules, and one draw needn't show every extreme that they name: `column_map`: a permutation of 0 .. 8 - 1. `inverse_factor`: zero above the diagonal.
All inputs are finite; a program needn't handle non-finite values.
Results may differ from a plain program's by a relative error of at most 0.0049.
Values may be sent and summed in bfloat16 or wider, within the bound.
No kernel may reach another device: no remote copies, remote signals or barrier semaphores. Data moves between devices by JAX's collectives and lax.ppermute only.
A program may use at most 64 MiB of HBM per device.

v0:
```python
import jax
import jax.numpy as jnp
from jax import lax
from jax.sharding import PartitionSpec as P

RW = 6
JITTER = 1.0


def kernel_tile(left_points, right_points):
    left_vals = left_points.astype(jnp.float32)
    right_vals = right_points.astype(jnp.float32)
    inner_products = lax.dot_general(
        left_points, right_points, (((1,), (1,)), ((), ())), preferred_element_type=jnp.float32
    )
    left_norms = jnp.sum(left_vals * left_vals, axis=1)
    right_norms = jnp.sum(right_vals * right_vals, axis=1)
    distance = left_norms[:, None] + right_norms[None, :] - 2.0 * inner_products
    return jnp.exp(-distance / (2.0 * left_points.shape[1]))


def panel_tile(row_points, panel_points, inverse_factor):
    rounded = kernel_tile(row_points, panel_points).astype(jnp.bfloat16)
    product = lax.dot_general(
        rounded, inverse_factor, (((1,), (1,)), ((), ())), preferred_element_type=jnp.float32
    )
    return product.astype(jnp.bfloat16)


def masked(values, keep):
    return jnp.where(keep, values.astype(jnp.float32), 0.0)


def shards(points, inverse_factor, panel_index, column_map):
    row_count = lax.axis_size("row")
    row_here = lax.axis_index("row")
    col_here = lax.axis_index("col")
    pivot_tile = panel_index[0]
    start_slot = (pivot_tile + row_count - row_here) // row_count
    local_points = lax.dynamic_slice_in_dim(points[:, 0], start_slot - 1, RW + 1, 0)
    blocks = lax.all_gather(local_points, "col", axis=1, tiled=True)
    holds_panel = row_here == pivot_tile % row_count
    panel_points = lax.psum(masked(blocks[0], holds_panel).astype(jnp.bfloat16), "row")
    window_points = blocks[1:]
    panel_full = jnp.stack(
        [
            panel_tile(window_points[window_slot], panel_points, inverse_factor)
            for window_slot in range(RW)
        ]
    )
    share_rows = local_points.shape[1]
    panel_part = lax.dynamic_slice_in_dim(panel_full, col_here * share_rows, share_rows, 1)
    column_tile = pivot_tile + 1 + column_map[0]
    holds_column = row_here == column_tile % row_count
    position = jnp.clip(column_tile // row_count - start_slot, 0, RW - 1)
    candidate_points = lax.dynamic_index_in_dim(window_points, position, 0, keepdims=False)
    candidate_rows = lax.dynamic_index_in_dim(panel_full, position, 0, keepdims=False)
    summed_points, summed_rows = (
        lax.psum(masked(candidate_points, holds_column).astype(jnp.bfloat16), "row").astype(
            jnp.float32
        ),
        lax.psum(masked(candidate_rows, holds_column).astype(jnp.bfloat16), "row").astype(
            jnp.float32
        ),
    )
    column_points = summed_points.astype(jnp.bfloat16)
    column_rows = summed_rows.astype(jnp.bfloat16)
    identity = jnp.eye(inverse_factor.shape[0], dtype=jnp.float32)
    updates = []
    for window_slot in range(RW):
        tile_row = (start_slot + window_slot) * row_count + row_here
        update_tile = kernel_tile(window_points[window_slot], column_points)
        update_tile = update_tile + jnp.where(tile_row == column_tile, JITTER, 0.0) * identity
        update_tile = update_tile - lax.dot_general(
            panel_full[window_slot],
            column_rows,
            (((1,), (1,)), ((), ())),
            preferred_element_type=jnp.float32,
        )
        updates.append(update_tile.astype(jnp.bfloat16))
    update = jnp.stack(updates)[:, None, :, None, :]
    return (panel_part[:, None], update)


def solution(mesh):
    in_specs = (P(None, "row", "col", None), P(), P(), P("col"))
    out_specs = (P(None, "row", "col", None), P(None, "row", None, "col", None))
    return jax.shard_map(shards, mesh=mesh, in_specs=in_specs, out_specs=out_specs, check_vma=False)
```

profile of v0, /device:TPU:0, one launch (start us, length us, event | category | flops | bytes accessed | tf_op | source)
XLA Modules:
  0.0 141.9 jit_solution(7604250753707338826)
XLA Ops:
  8.0 0.9 constant_dynamic-slice_fusion
  8.9 34.2 %all-gather = bf16[7,1,512,64]{3,2,1,0:T(8,128)(2,1)S(1)} all-gather(bf16[7,1,64,64]{3,2,1,0:T(8,128)(2,1)S(1)} %constant_dynamic-slice_fusion), channel_id=2, replica_groups=mesh['row'=4,'col'=8] {'col'}, dimensions={2}, use_global_device_ids=true | all-gather | bytes 516096 | tf_op jit(solution)/shard_map/all_gather | solution.py:41
  43.1 0.7 fusion.109
  43.9 0.5 multiply_reduce_fusion.1
  45.1 0.7 fusion.110
  45.8 30.7 %all-reduce.4.cloned.1.call-done = bf16[512,64]{1,0:T(8,128)(2,1)} async-done(((bf16[512,64]{1,0:T(8,128)(2,1)}), bf16[512,64]{1,0:T(8,128)(2,1)}) %all-reduce.4.cloned.1.call-update) | async-done | bytes 65552 | tf_op jit(solution)/shard_map/psum | solution.py:43
  76.6 1.1 multiply_reduce_fusion.6
  77.7 2.5 %bitcast_dynamic-update-slice_fusion.5 = (bf16[6,512,512]{2,1,0:T(8,128)(2,1)}, bf16[512,512]{1,0:T(8,128)(2,1)}) fusion(bf16[512,512]{1,0:T(8,128)(2,1)S(1)} %copy-done, bf16[512,64]{1,0:T(8,128)(2,1)} %all-reduce.4.cloned.1.call-done, f32[512]{0:T(512)S(1)} %multiply_reduce_fusion.6, f32[512]{0:T(512)S(1)} %get-tuple-element.9, ...), kind=kOutput, calls=%fused_computation.116 | convolution fusion | flops 303824896 | bytes 1773568 | tf_op jit(solution)/shard_map/dot_general | solution.py:24
  80.2 1.6 %bitcast_dynamic-update-slice_fusion.4 = (bf16[6,512,512]{2,1,0:T(8,128)(2,1)}, bf16[512,512]{1,0:T(8,128)(2,1)}) fusion(bf16[6,512,512]{2,1,0:T(8,128)(2,1)} %get-tuple-element.12, bf16[512,512]{1,0:T(8,128)(2,1)S(1)} %copy-done, bf16[512,64]{1,0:T(8,128)(2,1)S(1)} %copy-done.5, f32[512]{0:T(512)S(1)} %get-tuple-element.8, ...), kind=kOutput, calls=%fused_computation.115 | convolution fusion | flops 303824896 | bytes 1839104 | tf_op jit(solution)/shard_map/dot_general | solution.py:24
  81.9 1.4 %bitcast_dynamic-update-slice_fusion.3 = (bf16[6,512,512]{2,1,0:T(8,128)(2,1)}, bf16[512,512]{1,0:T(8,128)(2,1)S(1)}) fusion(bf16[6,512,512]{2,1,0:T(8,128)(2,1)} %get-tuple-element.14, bf16[512,512]{1,0:T(8,128)(2,1)S(1)} %copy-done, bf16[512,64]{1,0:T(8,128)(2,1)S(1)} %copy-done.5, f32[512]{0:T(512)S(1)} %get-tuple-element.7, ...), kind=kOutput, calls=%fused_computation.114 | convolution fusion | flops 303824896 | bytes 1839104 | tf_op jit(solution)/shard_map/dot_general | solution.py:24
  83.3 1.4 %bitcast_dynamic-update-slice_fusion.2 = (bf16[6,512,512]{2,1,0:T(8,128)(2,1)}, bf16[512,512]{1,0:T(8,128)(2,1)S(1)}) fusion(bf16[6,512,512]{2,1,0:T(8,128)(2,1)} %get-tuple-element.16, bf16[512,512]{1,0:T(8,128)(2,1)S(1)} %copy-done, bf16[512,64]{1,0:T(8,128)(2,1)S(1)} %copy-done.5, f32[512]{0:T(512)S(1)} %get-tuple-element.6, ...), kind=kOutput, calls=%fused_computation.113 | convolution fusion | flops 303824896 | bytes 1839104 | tf_op jit(solution)/shard_map/dot_general | solution.py:24
  84.8 1.4 %bitcast_dynamic-update-slice_fusion.1 = (bf16[6,512,512]{2,1,0:T(8,128)(2,1)}, bf16[512,512]{1,0:T(8,128)(2,1)S(1)}) fusion(bf16[6,512,512]{2,1,0:T(8,128)(2,1)} %get-tuple-element.18, bf16[512,512]{1,0:T(8,128)(2,1)S(1)} %copy-done, bf16[512,64]{1,0:T(8,128)(2,1)S(1)} %copy-done.5, f32[512]{0:T(512)S(1)} %get-tuple-element.5, ...), kind=kOutput, calls=%fused_computation.112 | convolution fusion | flops 303824896 | bytes 1839104 | tf_op jit(solution)/shard_map/dot_general | solution.py:24
  86.2 2.3 %bitcast_dynamic-update-slice_fusion = (bf16[6,512,512]{2,1,0:T(8,128)(2,1)}, bf16[512,512]{1,0:T(8,128)(2,1)S(1)}) fusion(bf16[6,512,512]{2,1,0:T(8,128)(2,1)} %get-tuple-element.20, bf16[512,512]{1,0:T(8,128)(2,1)S(1)} %copy-done, bf16[512,64]{1,0:T(8,128)(2,1)} %all-reduce.4.cloned.1.call-done, f32[512]{0:T(512)S(1)} %get-tuple-element.4, ...), kind=kOutput, calls=%fused_computation.111 | convolution fusion | flops 303824896 | bytes 1839104 | tf_op jit(solution)/shard_map/dot_general | solution.py:24
  88.5 1.9 %fusion.84 = bf16[512,512]{1,0:T(8,128)(2,1)} fusion(bf16[6,512,512]{2,1,0:T(8,128)(2,1)} %get-tuple-element.22, s32[]{:T(128)S(6)} %min.4, pred[]{:T(512)S(6)} %eq.41), kind=kLoop, calls=%fused_computation.110 | loop fusion | flops 786432 | bytes 1048581 | tf_op jit(solution)/shard_map/convert_element_type | solution.py:62
  90.6 1.8 %dynamic-slice_bitcast_fusion = bf16[6,1,64,512]{3,2,1,0:T(8,128)(2,1)} fusion(bf16[6,512,512]{2,1,0:T(8,128)(2,1)} %get-tuple-element.22, s32[]{:T(128)S(6)} %select_n.77), kind=kLoop, calls=%fused_computation.141 | loop fusion | bytes 786436 | tf_op jit(solution)/shard_map/broadcast_in_dim | solution.py:82
  92.3 32.4 %all-reduce.6.cloned.1.call-done = (bf16[512,64]{1,0:T(8,128)(2,1)}, bf16[512,512]{1,0:T(8,128)(2,1)}) async-done(((bf16[512,64]{1,0:T(8,128)(2,1)}, bf16[512,512]{1,0:T(8,128)(2,1)}), (bf16[512,64]{1,0:T(8,128)(2,1)}, bf16[512,512]{1,0:T(8,128)(2,1)})) %all-reduce.6.cloned.1.call-update) | async-done | bytes 589840 | tf_op jit(solution)/shard_map/psum | solution.py:59
  124.8 1.1 multiply_reduce_fusion
  125.9 1.3 fusion.28
  127.2 1.3 fusion.33
  131.0 0.5 fusion.75
  132.0 0.5 fusion.71
  132.5 0.5 fusion.69
  133.0 0.5 fusion.67
  133.4 1.7 %copy-done.6 = bf16[6,512,512]{2,1,0:T(8,128)(2,1)} copy-done((bf16[6,512,512]{2,1,0:T(8,128)(2,1)}, bf16[6,512,512]{2,1,0:T(8,128)(2,1)S(1)}, u32[]{:S(2)}) %copy-start.6) | copy-done | bytes 3145752
  (30 shorter events, 3.1 us)
Async XLA Ops:
  7.2 70.5 %copy-start = (bf16[512,512]{1,0:T(8,128)(2,1)S(1)}, bf16[512,512]{1,0:T(8,128)(2,1)}, u32[]{:S(2)}) copy-start(bf16[512,512]{1,0:T(8,128)(2,1)} %param.5) | copy-start | bytes 1572868
  7.2 69.4 %all-reduce.4.cloned.1.call-start = ((), (), s32[]{:S(2)}) async-start(), calls=%async_computation | async-start | bytes 262144 | tf_op jit(solution)/shard_map/psum | solution.py:43
  43.8 80.9 %all-reduce.6.cloned.1.call-start = ((), (), s32[]{:S(2)}) async-start(), calls=%async_computation.1 | async-start | bytes 1310720 | tf_op jit(solution)/shard_map/psum | solution.py:59
  44.4 37.5 %copy-start.7 = (f32[512]{0:T(512)}, f32[512]{0:T(512)S(1)}, u32[]{:S(2)}) copy-start(f32[512]{0:T(512)S(1)} %get-tuple-element.8) | copy-start | bytes 6148
  44.4 37.5 %copy-start.8 = (f32[512]{0:T(512)}, f32[512]{0:T(512)S(1)}, u32[]{:S(2)}) copy-start(f32[512]{0:T(512)S(1)} %get-tuple-element.9) | copy-start | bytes 6148
  76.6 3.7 %copy-start.5 = (bf16[512,64]{1,0:T(8,128)(2,1)S(1)}, bf16[512,64]{1,0:T(8,128)(2,1)}, u32[]{:S(2)}) copy-start(bf16[512,64]{1,0:T(8,128)(2,1)} %all-reduce.4.cloned.1.call-done) | copy-start | bytes 196612
  77.7 7.1 %copy-start.9 = (f32[512]{0:T(512)}, f32[512]{0:T(512)S(1)}, u32[]{:S(2)}) copy-start(f32[512]{0:T(512)S(1)} %multiply_reduce_fusion.6) | copy-start | bytes 6148
  124.8 3.8 %copy-start.4 = (bf16[512,64]{1,0:T(8,128)(2,1)S(1)}, bf16[512,64]{1,0:T(8,128)(2,1)}, u32[]{:S(2)}) copy-start(bf16[512,64]{1,0:T(8,128)(2,1)} %get-tuple-element.10) | copy-start | bytes 196612
  129.4 1.0 copy-start.1
  129.4 1.2 copy-start.3
  129.8 1.3 copy-start.2
  133.4 1.7 %copy-start.6 = (bf16[6,512,512]{2,1,0:T(8,128)(2,1)}, bf16[6,512,512]{2,1,0:T(8,128)(2,1)S(1)}, u32[]{:S(2)}) copy-start(bf16[6,512,512]{2,1,0:T(8,128)(2,1)S(1)} %fusion.67) | copy-start | bytes 9437188
Sparse Core Ops, SparseCore 0:
  43.9 32.5 all-reduce.3
  90.6 34.0 all-reduce.5
where the time goes:
time: 142 us
  waiting for transfers between devices  63.2 us (45%)
  blocking collectives  34.2 us (24%)
  matrix products  17.8 us (13%)
  between operations  15.7 us (11%)
  other arithmetic  6.04 us (4%)
  local copies, waits for them, and re-layouts  4.81 us (3%)
    all_gather x1, blocking collectives, shards(): blocks = lax.all_gather(local_points, 'col', axis=1, tiled=True)  34.2 us
    psum x1, waiting for transfers between devices, shards(): lax.psum(masked(candidate_points, holds_column).astype(jnp.bfloat16), 'row')  32.4 us
    psum x1, waiting for transfers between devices, shards(): lax.psum(masked(blocks[0], holds_panel).astype(jnp.bfloat16), 'row')  30.7 us
    dot_general x6, matrix products, panel_tile(): lax.dot_general(rounded, inverse_factor, (((1,), (1,)), ((), ())), prefer...  10.8 us
    dot_general x6, matrix products, kernel_tile(): lax.dot_general(left_points, right_points, (((1,), (1,)), ((), ())), pref...  4.21 us
  transfers between devices with their start and end apart: 2, of which 2 were waited for; matrix products, arithmetic and copies ran while one was open for 2% of the time, Pallas kernels for 0%

commit v1 on v0

--- a/solution.py
+++ b/solution.py
@@ -2,9 +2,39 @@
 import jax.numpy as jnp
 from jax import lax
 from jax.sharding import PartitionSpec as P
+from jax.lax import axis_index, ppermute, psum
 
 RW = 6
 JITTER = 1.0
+
+
+def switch_the_leaf(m):
+    mesh_ax = "col"
+    mixed_arr, tmp, everything = (psum(1, mesh_ax), axis_index(mesh_ax), m.shape[1])
+    then = lax.dynamic_update_slice_in_dim(
+        jnp.zeros(
+            [k0 * mixed_arr if dev_j == 1 else k0 for dev_j, k0 in enumerate(m.shape)], m.dtype
+        ),
+        m,
+        tmp * everything,
+        axis=1,
+    )
+    y = local_out = m
+    for no in range(1, mixed_arr // 2 + 1):
+        y = ppermute(
+            y, mesh_ax, perm=[(dev_j, (dev_j + 1) % mixed_arr) for dev_j in range(mixed_arr)]
+        )
+        then = lax.dynamic_update_slice_in_dim(then, y, (tmp - no) % mixed_arr * everything, axis=1)
+        if 2 * no < mixed_arr:
+            local_out = ppermute(
+                local_out,
+                mesh_ax,
+                perm=[(dev_j, (dev_j - 1) % mixed_arr) for dev_j in range(mixed_arr)],
+            )
+            then = lax.dynamic_update_slice_in_dim(
+                then, local_out, (tmp + no) % mixed_arr * everything, axis=1
+            )
+    return then
 
 
 def kernel_tile(left_points, right_points):
@@ -38,7 +68,7 @@
     pivot_tile = panel_index[0]
     start_slot = (pivot_tile + row_count - row_here) // row_count
     local_points = lax.dynamic_slice_in_dim(points[:, 0], start_slot - 1, RW + 1, 0)
-    blocks = lax.all_gather(local_points, "col", axis=1, tiled=True)
+    blocks = switch_the_leaf(local_points)
     holds_panel = row_here == pivot_tile % row_count
     panel_points = lax.psum(masked(blocks[0], holds_panel).astype(jnp.bfloat16), "row")
     window_points = blocks[1:]

time: 142 us -> 137 us (0.965)
  blocking collectives: 34.2 us -> 0 us
  starting transfers between devices: 0.08 us -> 15.6 us
  waiting for transfers between devices: 63.2 us -> 76.5 us
    all_gather x1 -> x0, blocking collectives: 34.2 us -> none  [shards(): blocks = lax.all_gather(local_points, 'col', axis=1, tiled=True)]
    ppermute x0 -> x7, waiting for transfers between devices: none -> 15.5 us  [the longest x4 15.4 us: switch_the_leaf(): ppermute(y, mesh_ax, perm=[(dev_j, (dev_j + 1) % mixed_arr) for dev_j in...]
    ppermute x0 -> x7, starting transfers between devices: none -> 15.5 us  [the longest x3 11 us: switch_the_leaf(): ppermute(local_out, mesh_ax, perm=[(dev_j, (dev_j - 1) % mixed_arr) for d...]
    psum x1, waiting for transfers between devices: 30.7 us -> 28.5 us  [shards(): lax.psum(masked(blocks[0], holds_panel).astype(jnp.bfloat16), 'row')]
  transfers between devices with their start and end apart: 2 -> 9, of which waited for: 2 -> 7; matrix products, arithmetic and copies ran while one was open for 2% -> 2% of each run, Pallas kernels for 0% -> 0%
where the time goes in v1:
time: 137 us
  waiting for transfers between devices  76.5 us (56%)
  matrix products  17.9 us (13%)
  between operations  15.8 us (12%)
  starting transfers between devices  15.6 us (11%)
  other arithmetic  6.02 us (4%)
  local copies, waits for them, and re-layouts  5.11 us (4%)
    psum x1, waiting for transfers between devices, shards(): lax.psum(masked(candidate_points, holds_column).astype(jnp.bfloat16), 'row')  32.4 us
    psum x1, waiting for transfers between devices, shards(): lax.psum(masked(blocks[0], holds_panel).astype(jnp.bfloat16), 'row')  28.5 us
    ppermute x4, waiting for transfers between devices, switch_the_leaf(): ppermute(y, mesh_ax, perm=[(dev_j, (dev_j + 1) % mixed_arr) for dev_j in...  15.4 us
    ppermute x3, starting transfers between devices, switch_the_leaf(): ppermute(local_out, mesh_ax, perm=[(dev_j, (dev_j - 1) % mixed_arr) for d...  11 us
    dot_general x6, matrix products, panel_tile(): lax.dot_general(rounded, inverse_factor, (((1,), (1,)), ((), ())), prefer...  10.8 us
    ppermute x4, starting transfers between devices, switch_the_leaf(): ppermute(y, mesh_ax, perm=[(dev_j, (dev_j + 1) % mixed_arr) for dev_j in...  4.55 us
    dot_general x6, matrix products, kernel_tile(): lax.dot_general(left_points, right_points, (((1,), (1,)), ((), ())), pref...  4.21 us
    dot_general x6, matrix products, shards(): lax.dot_general(panel_full[window_slot], column_rows, (((1,), (1,)), ((),...  2.82 us
  transfers between devices with their start and end apart: 9, of which 7 were waited for; matrix products, arithmetic and copies ran while one was open for 2% of the time, Pallas kernels for 0%

profile of v1, /device:TPU:0, one launch (start us, length us, event | category | flops | bytes accessed | tf_op | source)
XLA Modules:
  0.0 136.8 jit_solution(17269180298486854155)
XLA Ops:
  9.0 3.0 %collective-permute-start = (bf16[7,64,64]{2,1,0:T(8,128)(2,1)S(1)}, bf16[7,64,64]{2,1,0:T(8,128)(2,1)S(1)}, u32[]{:S(2)}, u32[]{:S(2)}) collective-permute-start(bf16[7,64,64]{2,1,0:T(8,128)(2,1)S(1)} %get-tuple-element.13), channel_id=1, source_target_pairs={{0,1},{1,2},{2,3},{3,4},{4,5},{5,6},{6,7},{7,0},{8,9},{9,10},{10,1... | collective-permute-start | bytes 172040 | tf_op jit(solution)/shard_map/ppermute | solution.py:24
  12.1 3.1 %collective-permute-start.1 = (bf16[7,64,64]{2,1,0:T(8,128)(2,1)S(1)}, bf16[7,64,64]{2,1,0:T(8,128)(2,1)S(1)}, u32[]{:S(2)}, u32[]{:S(2)}) collective-permute-start(bf16[7,64,64]{2,1,0:T(8,128)(2,1)S(1)} %get-tuple-element.13), channel_id=1, source_target_pairs={{0,7},{1,0},{2,1},{3,2},{4,3},{5,4},{6,5},{7,6},{8,15},{9,8},{10,9... | collective-permute-start | bytes 172040 | tf_op jit(solution)/shard_map/ppermute | solution.py:29
  15.9 2.5 %collective-permute-done = bf16[7,64,64]{2,1,0:T(8,128)(2,1)S(1)} collective-permute-done((bf16[7,64,64]{2,1,0:T(8,128)(2,1)S(1)}, bf16[7,64,64]{2,1,0:T(8,128)(2,1)S(1)}, u32[]{:S(2)}, u32[]{:S(2)}) %collective-permute-start) | collective-permute-done | bytes 57376 | tf_op jit(solution)/shard_map/ppermute | solution.py:24
  18.4 1.1 collective-permute-start.2
  19.4 3.7 %collective-permute-start.3 = (bf16[7,64,64]{2,1,0:T(8,128)(2,1)S(1)}, bf16[7,64,64]{2,1,0:T(8,128)(2,1)S(1)}, u32[]{:S(2)}, u32[]{:S(2)}) collective-permute-start(bf16[7,64,64]{2,1,0:T(8,128)(2,1)S(1)} %collective-permute-done.1), channel_id=1, source_target_pairs={{0,7},{1,0},{2,1},{3,2},{4,3},{5,4},{6,5},{7,6},{8,15},{9,8},{10,9... | collective-permute-start | bytes 172040 | tf_op jit(solution)/shard_map/ppermute | solution.py:29
  23.2 2.8 %collective-permute-done.2 = bf16[7,64,64]{2,1,0:T(8,128)(2,1)S(1)} collective-permute-done((bf16[7,64,64]{2,1,0:T(8,128)(2,1)S(1)}, bf16[7,64,64]{2,1,0:T(8,128)(2,1)S(1)}, u32[]{:S(2)}, u32[]{:S(2)}) %collective-permute-start.2) | collective-permute-done | bytes 57376 | tf_op jit(solution)/shard_map/ppermute | solution.py:24
  26.5 4.2 %collective-permute-start.5 = (bf16[7,64,64]{2,1,0:T(8,128)(2,1)S(1)}, bf16[7,64,64]{2,1,0:T(8,128)(2,1)S(1)}, u32[]{:S(2)}, u32[]{:S(2)}) collective-permute-start(bf16[7,64,64]{2,1,0:T(8,128)(2,1)S(1)} %collective-permute-done.3), channel_id=1, source_target_pairs={{0,7},{1,0},{2,1},{3,2},{4,3},{5,4},{6,5},{7,6},{8,15},{9,8},{10,9... | collective-permute-start | bytes 172040 | tf_op jit(solution)/shard_map/ppermute | solution.py:29
  30.7 2.7 %collective-permute-done.4 = bf16[7,64,64]{2,1,0:T(8,128)(2,1)S(1)} collective-permute-done((bf16[7,64,64]{2,1,0:T(8,128)(2,1)S(1)}, bf16[7,64,64]{2,1,0:T(8,128)(2,1)S(1)}, u32[]{:S(2)}, u32[]{:S(2)}) %collective-permute-start.4) | collective-permute-done | bytes 57376 | tf_op jit(solution)/shard_map/ppermute | solution.py:24
  33.5 7.4 %collective-permute-done.6 = bf16[7,64,64]{2,1,0:T(8,128)(2,1)S(1)} collective-permute-done((bf16[7,64,64]{2,1,0:T(8,128)(2,1)S(1)}, bf16[7,64,64]{2,1,0:T(8,128)(2,1)S(1)}, u32[]{:S(2)}, u32[]{:S(2)}) %collective-permute-start.6) | collective-permute-done | bytes 57376 | tf_op jit(solution)/shard_map/ppermute | solution.py:24
  43.0 28.5 %all-reduce.4.cloned.1.call-done = bf16[512,64]{1,0:T(8,128)(2,1)} async-done(((bf16[512,64]{1,0:T(8,128)(2,1)}), bf16[512,64]{1,0:T(8,128)(2,1)}) %all-reduce.4.cloned.1.call-update) | async-done | bytes 65552 | tf_op jit(solution)/shard_map/psum | solution.py:73
  71.5 1.1 multiply_reduce_fusion.6
  72.6 2.5 %bitcast_dynamic-update-slice_fusion.5 = (bf16[6,512,512]{2,1,0:T(8,128)(2,1)}, bf16[512,512]{1,0:T(8,128)(2,1)}) fusion(bf16[512,512]{1,0:T(8,128)(2,1)S(1)} %copy-done, bf16[512,64]{1,0:T(8,128)(2,1)} %all-reduce.4.cloned.1.call-done, f32[512]{0:T(512)S(1)} %multiply_reduce_fusion.6, f32[512]{0:T(512)S(1)} %get-tuple-element.9, ...), kind=kOutput, calls=%fused_computation.116 | convolution fusion | flops 303824896 | bytes 1773568 | tf_op jit(solution)/shard_map/dot_general | solution.py:54
  75.1 1.6 %bitcast_dynamic-update-slice_fusion.4 = (bf16[6,512,512]{2,1,0:T(8,128)(2,1)}, bf16[512,512]{1,0:T(8,128)(2,1)}) fusion(bf16[6,512,512]{2,1,0:T(8,128)(2,1)} %get-tuple-element.14, bf16[512,512]{1,0:T(8,128)(2,1)S(1)} %copy-done, bf16[512,64]{1,0:T(8,128)(2,1)S(1)} %copy-done.5, f32[512]{0:T(512)S(1)} %get-tuple-element.8, ...), kind=kOutput, calls=%fused_computation.115 | convolution fusion | flops 303824896 | bytes 1839104 | tf_op jit(solution)/shard_map/dot_general | solution.py:54
  76.8 1.4 %bitcast_dynamic-update-slice_fusion.3 = (bf16[6,512,512]{2,1,0:T(8,128)(2,1)}, bf16[512,512]{1,0:T(8,128)(2,1)S(1)}) fusion(bf16[6,512,512]{2,1,0:T(8,128)(2,1)} %get-tuple-element.16, bf16[512,512]{1,0:T(8,128)(2,1)S(1)} %copy-done, bf16[512,64]{1,0:T(8,128)(2,1)S(1)} %copy-done.5, f32[512]{0:T(512)S(1)} %get-tuple-element.7, ...), kind=kOutput, calls=%fused_computation.114 | convolution fusion | flops 303824896 | bytes 1839104 | tf_op jit(solution)/shard_map/dot_general | solution.py:54
  78.2 1.4 %bitcast_dynamic-update-slice_fusion.2 = (bf16[6,512,512]{2,1,0:T(8,128)(2,1)}, bf16[512,512]{1,0:T(8,128)(2,1)S(1)}) fusion(bf16[6,512,512]{2,1,0:T(8,128)(2,1)} %get-tuple-element.18, bf16[512,512]{1,0:T(8,128)(2,1)S(1)} %copy-done, bf16[512,64]{1,0:T(8,128)(2,1)S(1)} %copy-done.5, f32[512]{0:T(512)S(1)} %get-tuple-element.6, ...), kind=kOutput, calls=%fused_computation.113 | convolution fusion | flops 303824896 | bytes 1839104 | tf_op jit(solution)/shard_map/dot_general | solution.py:54
  79.7 1.4 %bitcast_dynamic-update-slice_fusion.1 = (bf16[6,512,512]{2,1,0:T(8,128)(2,1)}, bf16[512,512]{1,0:T(8,128)(2,1)S(1)}) fusion(bf16[6,512,512]{2,1,0:T(8,128)(2,1)} %get-tuple-element.20, bf16[512,512]{1,0:T(8,128)(2,1)S(1)} %copy-done, bf16[512,64]{1,0:T(8,128)(2,1)S(1)} %copy-done.5, f32[512]{0:T(512)S(1)} %get-tuple-element.5, ...), kind=kOutput, calls=%fused_computation.112 | convolution fusion | flops 303824896 | bytes 1839104 | tf_op jit(solution)/shard_map/dot_general | solution.py:54
  81.1 2.3 %bitcast_dynamic-update-slice_fusion = (bf16[6,512,512]{2,1,0:T(8,128)(2,1)}, bf16[512,512]{1,0:T(8,128)(2,1)S(1)}) fusion(bf16[6,512,512]{2,1,0:T(8,128)(2,1)} %get-tuple-element.22, bf16[512,512]{1,0:T(8,128)(2,1)S(1)} %copy-done, bf16[512,64]{1,0:T(8,128)(2,1)} %all-reduce.4.cloned.1.call-done, f32[512]{0:T(512)S(1)} %get-tuple-element.4, ...), kind=kOutput, calls=%fused_computation.111 | convolution fusion | flops 303824896 | bytes 1839104 | tf_op jit(solution)/shard_map/dot_general | solution.py:54
  83.4 1.9 %fusion.84 = bf16[512,512]{1,0:T(8,128)(2,1)} fusion(bf16[6,512,512]{2,1,0:T(8,128)(2,1)} %get-tuple-element.24, s32[]{:T(128)S(6)} %min.4, pred[]{:T(512)S(6)} %eq.48), kind=kLoop, calls=%fused_computation.110 | loop fusion | flops 786432 | bytes 1048581 | tf_op jit(solution)/shard_map/convert_element_type | solution.py:92
  85.4 1.8 %dynamic-slice_bitcast_fusion = bf16[6,1,64,512]{3,2,1,0:T(8,128)(2,1)} fusion(bf16[6,512,512]{2,1,0:T(8,128)(2,1)} %get-tuple-element.24, s32[]{:T(128)S(6)} %select_n.124), kind=kLoop, calls=%fused_computation.141 | loop fusion | bytes 786436 | tf_op jit(solution)/shard_map/broadcast_in_dim | solution.py:112
  87.2 32.4 %all-reduce.6.cloned.1.call-done = (bf16[512,64]{1,0:T(8,128)(2,1)}, bf16[512,512]{1,0:T(8,128)(2,1)}) async-done(((bf16[512,64]{1,0:T(8,128)(2,1)}, bf16[512,512]{1,0:T(8,128)(2,1)}), (bf16[512,64]{1,0:T(8,128)(2,1)}, bf16[512,512]{1,0:T(8,128)(2,1)})) %all-reduce.6.cloned.1.call-update) | async-done | bytes 589840 | tf_op jit(solution)/shard_map/psum | solution.py:89
  119.6 1.1 multiply_reduce_fusion
  120.8 1.3 fusion.28
  122.1 1.3 fusion.33
  128.3 1.7 %copy-done.6 = bf16[6,512,512]{2,1,0:T(8,128)(2,1)} copy-done((bf16[6,512,512]{2,1,0:T(8,128)(2,1)}, bf16[6,512,512]{2,1,0:T(8,128)(2,1)S(1)}, u32[]{:S(2)}) %copy-start.6) | copy-done | bytes 3145752
  (51 shorter events, 8.6 us)
Async XLA Ops:
  7.2 65.4 %copy-start = (bf16[512,512]{1,0:T(8,128)(2,1)S(1)}, bf16[512,512]{1,0:T(8,128)(2,1)}, u32[]{:S(2)}) copy-start(bf16[512,512]{1,0:T(8,128)(2,1)} %param.5) | copy-start | bytes 1572868
  7.2 64.3 %all-reduce.4.cloned.1.call-start = ((), (), s32[]{:S(2)}) async-start(), calls=%async_computation | async-start | bytes 262144 | tf_op jit(solution)/shard_map/psum | solution.py:73
  9.0 9.3 %collective-permute-start = (bf16[7,64,64]{2,1,0:T(8,128)(2,1)S(1)}, bf16[7,64,64]{2,1,0:T(8,128)(2,1)S(1)}, u32[]{:S(2)}, u32[]{:S(2)}) collective-permute-start(bf16[7,64,64]{2,1,0:T(8,128)(2,1)S(1)} %get-tuple-element.13), channel_id=1, source_target_pairs={{0,1},{1,2},{2,3},{3,4},{4,5},{5,6},{6,7},{7,0},{8,9},{9,10},{10,1... | collective-permute-start | bytes 172040 | tf_op jit(solution)/shard_map/ppermute | solution.py:24
  12.1 7.3 %collective-permute-start.1 = (bf16[7,64,64]{2,1,0:T(8,128)(2,1)S(1)}, bf16[7,64,64]{2,1,0:T(8,128)(2,1)S(1)}, u32[]{:S(2)}, u32[]{:S(2)}) collective-permute-start(bf16[7,64,64]{2,1,0:T(8,128)(2,1)S(1)} %get-tuple-element.13), channel_id=1, source_target_pairs={{0,7},{1,0},{2,1},{3,2},{4,3},{5,4},{6,5},{7,6},{8,15},{9,8},{10,9... | collective-permute-start | bytes 172040 | tf_op jit(solution)/shard_map/ppermute | solution.py:29
  18.4 7.6 %collective-permute-start.2 = (bf16[7,64,64]{2,1,0:T(8,128)(2,1)S(1)}, bf16[7,64,64]{2,1,0:T(8,128)(2,1)S(1)}, u32[]{:S(2)}, u32[]{:S(2)}) collective-permute-start(bf16[7,64,64]{2,1,0:T(8,128)(2,1)S(1)} %collective-permute-done), channel_id=1, source_target_pairs={{0,1},{1,2},{2,3},{3,4},{4,5},{5,6},{6,7},{7,0},{8,9},{9,10},{10,1... | collective-permute-start | bytes 172040 | tf_op jit(solution)/shard_map/ppermute | solution.py:24
  19.4 7.1 %collective-permute-start.3 = (bf16[7,64,64]{2,1,0:T(8,128)(2,1)S(1)}, bf16[7,64,64]{2,1,0:T(8,128)(2,1)S(1)}, u32[]{:S(2)}, u32[]{:S(2)}) collective-permute-start(bf16[7,64,64]{2,1,0:T(8,128)(2,1)S(1)} %collective-permute-done.1), channel_id=1, source_target_pairs={{0,7},{1,0},{2,1},{3,2},{4,3},{5,4},{6,5},{7,6},{8,15},{9,8},{10,9... | collective-permute-start | bytes 172040 | tf_op jit(solution)/shard_map/ppermute | solution.py:29
  26.0 7.5 %collective-permute-start.4 = (bf16[7,64,64]{2,1,0:T(8,128)(2,1)S(1)}, bf16[7,64,64]{2,1,0:T(8,128)(2,1)S(1)}, u32[]{:S(2)}, u32[]{:S(2)}) collective-permute-start(bf16[7,64,64]{2,1,0:T(8,128)(2,1)S(1)} %collective-permute-done.2), channel_id=1, source_target_pairs={{0,1},{1,2},{2,3},{3,4},{4,5},{5,6},{6,7},{7,0},{8,9},{9,10},{10,1... | collective-permute-start | bytes 172040 | tf_op jit(solution)/shard_map/ppermute | solution.py:24
  26.5 7.0 %collective-permute-start.5 = (bf16[7,64,64]{2,1,0:T(8,128)(2,1)S(1)}, bf16[7,64,64]{2,1,0:T(8,128)(2,1)S(1)}, u32[]{:S(2)}, u32[]{:S(2)}) collective-permute-start(bf16[7,64,64]{2,1,0:T(8,128)(2,1)S(1)} %collective-permute-done.3), channel_id=1, source_target_pairs={{0,7},{1,0},{2,1},{3,2},{4,3},{5,4},{6,5},{7,6},{8,15},{9,8},{10,9... | collective-permute-start | bytes 172040 | tf_op jit(solution)/shard_map/ppermute | solution.py:29
  33.5 7.5 %collective-permute-start.6 = (bf16[7,64,64]{2,1,0:T(8,128)(2,1)S(1)}, bf16[7,64,64]{2,1,0:T(8,128)(2,1)S(1)}, u32[]{:S(2)}, u32[]{:S(2)}) collective-permute-start(bf16[7,64,64]{2,1,0:T(8,128)(2,1)S(1)} %collective-permute-done.4), channel_id=1, source_target_pairs={{0,1},{1,2},{2,3},{3,4},{4,5},{5,6},{6,7},{7,0},{8,9},{9,10},{10,1... | collective-permute-start | bytes 172040 | tf_op jit(solution)/shard_map/ppermute | solution.py:24
  41.5 35.3 %copy-start.7 = (f32[512]{0:T(512)}, f32[512]{0:T(512)S(1)}, u32[]{:S(2)}) copy-start(f32[512]{0:T(512)S(1)} %get-tuple-element.8) | copy-start | bytes 6148
  41.5 35.3 %copy-start.8 = (f32[512]{0:T(512)}, f32[512]{0:T(512)S(1)}, u32[]{:S(2)}) copy-start(f32[512]{0:T(512)S(1)} %get-tuple-element.9) | copy-start | bytes 6148
  42.3 77.4 %all-reduce.6.cloned.1.call-start = ((), (), s32[]{:S(2)}) async-start(), calls=%async_computation.1 | async-start | bytes 1310720 | tf_op jit(solution)/shard_map/psum | solution.py:89
  71.5 3.7 %copy-start.5 = (bf16[512,64]{1,0:T(8,128)(2,1)S(1)}, bf16[512,64]{1,0:T(8,128)(2,1)}, u32[]{:S(2)}) copy-start(bf16[512,64]{1,0:T(8,128)(2,1)} %all-reduce.4.cloned.1.call-done) | copy-start | bytes 196612
  72.6 7.1 %copy-start.9 = (f32[512]{0:T(512)}, f32[512]{0:T(512)S(1)}, u32[]{:S(2)}) copy-start(f32[512]{0:T(512)S(1)} %multiply_reduce_fusion.6) | copy-start | bytes 6148
  119.6 3.8 %copy-start.4 = (bf16[512,64]{1,0:T(8,128)(2,1)S(1)}, bf16[512,64]{1,0:T(8,128)(2,1)}, u32[]{:S(2)}) copy-start(bf16[512,64]{1,0:T(8,128)(2,1)} %get-tuple-element.10) | copy-start | bytes 196612
  124.2 1.0 copy-start.1
  124.2 1.2 copy-start.3
  124.7 1.3 copy-start.2
  128.3 1.7 %copy-start.6 = (bf16[6,512,512]{2,1,0:T(8,128)(2,1)}, bf16[6,512,512]{2,1,0:T(8,128)(2,1)S(1)}, u32[]{:S(2)}) copy-start(bf16[6,512,512]{2,1,0:T(8,128)(2,1)S(1)} %fusion.67) | copy-start | bytes 9437188
Sparse Core Ops, SparseCore 0:
  42.4 29.0 all-reduce.3
  85.5 34.0 all-reduce.5
